TPU v7x, 768 devices: a whole 4x8x12 slice. The times are simulated.
768 devices in a mesh: group: 16 (over z_lo, x), fsdp: 48 (over z_hi, y, core).
Axes of the slice: x: 4, y: 8, z: 12 (z_hi: 3, z_lo: 4; z = z_hi * 4 + z_lo), core: 2. Of those that a mesh axis runs over, the one named last changes fastest.
Arguments:
- hidden_input_slots: bfloat16 [4096, 8192], P('group'), may hold values from -6 to 6
- base_weight: bfloat16 [8192, 14784], P('group', 'fsdp'), may hold values from -0.0625 to 0.0625
- adapter_a: bfloat16 [8192, 64], P('group'), may hold values from -0.0625 to 0.0625
- adapter_up_matrix: bfloat16 [64, 14784], P(None, 'fsdp'), may hold values from -0.75 to 0.75
- upstream: bfloat16 [4096, 14784], P('group', 'fsdp'), may hold values from -6 to 6
- logp_new: float32 [16, 16, 16], P('group'), may hold values from -2 to -0.5
- logp_old: float32 [16, 16, 16], P('group'), may hold values from -2 to -0.5
- rewards: float32 [16, 16], P('group'), may hold values from -1.35 to 2.35
- comp_lengths: int32 [16, 16], P('group'), may hold values from 1 to 16, 160 in all within a row
- assignment: int32 [16, 16], P('group'), may hold values from 0 to 15, each once within a row
Outputs:
- projection_output: bfloat16 [4096, 14784], P('group', 'fsdp')
- gradient_down_adapter: float32 [8192, 64], P('group')
- gradient_up_adapter: float32 [64, 14784], P('group', 'fsdp')
- loss_parts: float32 [16], P('group')
Inputs may be any that keep to these rules, and one draw needn't show every extreme that they name: `comp_lengths`: every generator group has a completion of exactly 16 tokens. `assignment`: each generator group assigns exactly one completion to each trainer group.
All inputs are finite; a program needn't handle non-finite values.
Results may differ from a plain program's by a relative error of at most 0.0049.
Values may be sent and summed in bfloat16 or wider, within the bound.
A program may use at most 64 MiB of HBM per device.

v0:
```python
import jax
import jax.numpy as jnp
from jax import lax
from jax.sharding import PartitionSpec as P

COMP = 16


ADAPTER_SCALING = 0.25
SPREAD_FLOOR = 0.16


def prompt_table(prompt_row, count):
    return (prompt_row[:, None] == jnp.arange(count, dtype=jnp.int32)[None, :]).astype(jnp.float32)


def advantages(reward_row, onehot, reward_sums, reward_squares):
    reward_mean = reward_sums / COMP
    reward_var = reward_squares / COMP - reward_mean * reward_mean
    spread = jnp.sqrt(jnp.maximum(reward_var, SPREAD_FLOOR))
    centre = jnp.dot(onehot, reward_mean, precision=lax.Precision.HIGHEST)
    scaled = jnp.dot(onehot, spread, precision=lax.Precision.HIGHEST)
    return (reward_row - centre) / scaled


def prompt_sums(reward_row, onehot):
    reward_sums = jnp.dot(reward_row, onehot, precision=lax.Precision.HIGHEST)
    reward_squares = jnp.dot(reward_row * reward_row, onehot, precision=lax.Precision.HIGHEST)
    return (reward_sums, reward_squares)


def add_rows(hidden_input_slots, weight_piece):
    return jnp.dot(hidden_input_slots, weight_piece, preferred_element_type=jnp.float32)


def on_device(
    hidden_input_slots,
    base_weight,
    adapter_a,
    adapter_up_matrix,
    upstream,
    logp_new,
    logp_old,
    rewards,
    comp_lengths,
    assignment,
):
    groups = lax.axis_size("group")
    prompts = groups * groups // COMP
    own_group = lax.axis_index("group")
    prompt_row = (own_group * groups + jnp.arange(groups, dtype=jnp.int32)) // COMP
    dest_order = (assignment[0][None, :] == jnp.arange(groups, dtype=jnp.int32)[:, None]).astype(
        jnp.float32
    )
    send_old = jnp.dot(dest_order, logp_old[0], precision=lax.Precision.HIGHEST)
    send_len = jnp.dot(
        dest_order, comp_lengths[0].astype(jnp.float32), precision=lax.Precision.HIGHEST
    )
    reward_row = rewards[0]
    onehot = prompt_table(prompt_row, prompts)
    reward_sums, reward_squares = lax.psum(prompt_sums(reward_row, onehot), "group")
    advantage = advantages(reward_row, onehot, reward_sums, reward_squares)
    send_adv = jnp.dot(dest_order, advantage, precision=lax.Precision.HIGHEST)
    recv_old, recv_adv, recv_len = (
        lax.all_to_all(send_old, "group", split_axis=0, concat_axis=0, tiled=True),
        lax.all_to_all(send_adv, "group", split_axis=0, concat_axis=0, tiled=True),
        lax.all_to_all(send_len, "group", split_axis=0, concat_axis=0, tiled=True),
    )
    positions = jnp.arange(logp_new.shape[2]).astype(jnp.float32)
    live_mask = positions[None, :] < recv_len[:, None]
    prob_ratio = jnp.exp(logp_new[0] - recv_old)
    token_coef = jnp.where(
        live_mask, -(recv_adv[:, None] * prob_ratio) / (recv_len[:, None] * COMP), 0.0
    )
    loss_part = jnp.sum(token_coef)[None]
    output_gradient = (token_coef.reshape(-1, 1) * upstream.astype(jnp.float32)).astype(
        jnp.bfloat16
    )
    full_adapter = lax.all_gather(adapter_a, "group", axis=0, tiled=True)
    low_sum = jnp.dot(hidden_input_slots, full_adapter, preferred_element_type=jnp.float32)
    frozen_base_total = add_rows(
        hidden_input_slots, lax.all_gather(base_weight, "group", axis=0, tiled=True)
    )
    reduced_rank_product = low_sum.astype(jnp.bfloat16)
    projection_output = (
        frozen_base_total
        + ADAPTER_SCALING
        * jnp.dot(reduced_rank_product, adapter_up_matrix, preferred_element_type=jnp.float32)
    ).astype(jnp.bfloat16)
    gradient_up_partial = ADAPTER_SCALING * lax.dot_general(
        reduced_rank_product,
        output_gradient,
        (((0,), (0,)), ((), ())),
        preferred_element_type=jnp.float32,
    )
    back_part = lax.dot_general(
        output_gradient,
        adapter_up_matrix,
        (((1,), (1,)), ((), ())),
        preferred_element_type=jnp.float32,
    )
    backward_lowrank = lax.psum(back_part, "fsdp").astype(jnp.bfloat16)
    gradient_down_partial = ADAPTER_SCALING * lax.dot_general(
        hidden_input_slots,
        backward_lowrank,
        (((0,), (0,)), ((), ())),
        preferred_element_type=jnp.float32,
    )
    gradient_down_adapter, gradient_up_adapter = (
        lax.psum_scatter(gradient_down_partial, "group", scatter_dimension=0, tiled=True),
        lax.psum_scatter(gradient_up_partial, "group", scatter_dimension=0, tiled=True),
    )
    return (projection_output, gradient_down_adapter, gradient_up_adapter, loss_part)


def solution(mesh):
    return jax.shard_map(
        on_device,
        mesh=mesh,
        in_specs=(
            P("group", None),
            P("group", "fsdp"),
            P("group", None),
            P(None, "fsdp"),
            P("group", "fsdp"),
            P("group", None, None),
            P("group", None, None),
            P("group", None),
            P("group", None),
            P("group", None),
        ),
        out_specs=(P("group", "fsdp"), P("group", None), P("group", "fsdp"), P("group")),
        check_vma=False,
    )
```

profile of v0, /device:TPU:8, one launch (start us, length us, event | category | flops | bytes accessed | tf_op | source)
XLA Modules:
  0.0 473.0 jit_solution(18351601305106989599)
XLA Ops:
  7.2 0.7 all-gather.5.cloned.1.call-update
  7.9 1.4 fusion.16
  9.3 9.8 %all-to-all-start = ((f32[16,1,1]{2,1,0:T(1,128)}), f32[16,1,1]{2,1,0:T(1,128)S(1)}, u32[]{:S(2)}, u32[]{:S(2)}) async-start(f32[16,1,1]{2,1,0:T(1,128)} %bitcast.28), calls=%async_computation | async-start | bytes 16384 | tf_op jit(solution)/shard_map/all_to_all | solution.py:67
  19.2 0.8 convolution_bitcast_fusion.1
  20.0 0.8 convolution_bitcast_fusion.3
  20.9 43.6 %all-reduce.1 = (f32[16]{0:T(128)S(1)}, f32[16]{0:T(128)S(1)}) all-reduce(f32[16]{0:T(128)S(1)} %convolution_bitcast_fusion.1, f32[16]{0:T(128)S(1)} %convolution_bitcast_fusion.3), channel_id=1, replica_groups=mesh['group'=16,'fsdp'=48] {'group'}, use_global_device_ids=true, to_apply=%region_1.2 | all-reduce | flops 32 | bytes 256 | tf_op jit(solution)/shard_map/psum | solution.py:61
  64.5 0.2 convolution_bitcast_fusion
  64.7 0.9 fusion.5
  65.6 1.4 fusion.15
  67.0 1.4 fusion.13
  68.4 0.8 squeeze.13
  69.2 3.5 all-to-all-start.1
  72.7 0.2 reduce
  72.9 7.5 %all-to-all-done.1 = f32[16,1,1]{2,1,0:T(1,128)S(1)} async-done(((f32[16,1,1]{2,1,0:T(1,128)}), f32[16,1,1]{2,1,0:T(1,128)S(1)}, u32[]{:S(2)}, u32[]{:S(2)}) %all-to-all-start.1) | async-done | bytes 96 | tf_op jit(solution)/shard_map/all_to_all | solution.py:66
  80.5 3.5 all-to-all-start.2
  84.3 0.2 reduce.1
  84.6 7.2 %all-to-all-done.2 = f32[16,1,16]{2,1,0:T(1,128)S(1)} async-done(((f32[16,1,16]{2,1,0:T(1,128)}), f32[16,1,16]{2,1,0:T(1,128)S(1)}, u32[]{:S(2)}, u32[]{:S(2)}) %all-to-all-start.2) | async-done | bytes 1056 | tf_op jit(solution)/shard_map/all_to_all | solution.py:65
  91.9 0.5 broadcast.93
  92.4 0.7 reduce.5
  93.2 10.5 %all-gather.5.cloned.1.call-done = bf16[8192,64]{0,1:T(8,128)(2,1)} async-done(((bf16[512,64]{0,1:T(8,128)(2,1)}), bf16[8192,64]{0,1:T(8,128)(2,1)}) %all-gather.5.cloned.1.call-update) | async-done | bytes 1048592 | tf_op jit(solution)/shard_map/all_gather | solution.py:79
  103.7 3.9 convolution_convert_fusion
  107.6 0.8 convolution_multiply_fusion.2
  108.5 0.7 all-gather.3.cloned.1.call-update
  109.4 243.4 %psum.23 = bf16[256,64]{0,1:T(8,128)(2,1)S(1)} all-reduce(f32[256,64]{0,1:T(8,128)S(1)} %fusion.6), channel_id=1, replica_groups=mesh['group'=16,'fsdp'=48] {'fsdp'}, use_global_device_ids=true, to_apply=%region_2.3 | all-reduce | flops 16384 | bytes 98304 | tf_op jit(solution)/shard_map/psum | solution.py:102
  352.8 4.5 fusion
  357.3 1.3 dynamic-slice
  359.2 0.7 fusion.17
  359.9 1.3 constant_dynamic-slice_fusion
  361.2 8.1 %all-gather.3.cloned.1.call-done = bf16[8192,308]{0,1:T(8,128)(2,1)} async-done(((bf16[512,308]{0,1:T(8,128)(2,1)}), bf16[8192,308]{0,1:T(8,128)(2,1)}) %all-gather.3.cloned.1.call-update) | async-done | bytes 5046288 | tf_op jit(solution)/shard_map/all_gather | solution.py:82
  369.3 5.3 %fusion.44 = f32[256,308]{0,1:T(8,128)S(1)} fusion(bf16[256,8192]{1,0:T(8,128)(2,1)} %param.10, bf16[8192,308]{0,1:T(8,128)(2,1)} %all-gather.3.cloned.1.call-done), kind=kOutput, calls=%fused_computation.66 | convolution fusion | flops 1291845632 | bytes 9555968 | tf_op jit(solution)/shard_map/dot_general | solution.py:33
  374.6 0.9 fusion.2
  375.5 90.9 %reduce-scatter.2.cloned.1.call-done = f32[512,64]{0,1:T(8,128)} async-done(((f32[8192,64]{0,1:T(8,128)}), f32[512,64]{0,1:T(8,128)}) %reduce-scatter.2.cloned.1.call-update) | async-done | bytes 131088 | tf_op jit(solution)/shard_map/reduce_scatter | solution.py:110
  (26 shorter events, 1.0 us)
Async XLA Ops:
  7.2 102.1 %copy-start = (bf16[64,308]{1,0:T(8,128)(2,1)S(1)}, bf16[64,308]{1,0:T(8,128)(2,1)}, u32[]{:S(2)}) copy-start(bf16[64,308]{1,0:T(8,128)(2,1)} %param.13) | copy-start | bytes 118276
  7.2 100.4 %copy-start.1 = (bf16[256,308]{0,1:T(8,128)(2,1)S(1)}, bf16[256,308]{0,1:T(8,128)(2,1)}, u32[]{:S(2)}) copy-start(bf16[256,308]{0,1:T(8,128)(2,1)} %param.14) | copy-start | bytes 473092
  7.2 96.5 %all-gather.5.cloned.1.call-start = ((), (), s32[]{:S(2)}) async-start(), calls=%async_computation.5 | async-start | bytes 1114112 | tf_op jit(solution)/shard_map/all_gather | solution.py:79
  9.3 59.8 %all-to-all-start = ((f32[16,1,1]{2,1,0:T(1,128)}), f32[16,1,1]{2,1,0:T(1,128)S(1)}, u32[]{:S(2)}, u32[]{:S(2)}) async-start(f32[16,1,1]{2,1,0:T(1,128)} %bitcast.28), calls=%async_computation | async-start | bytes 16384 | tf_op jit(solution)/shard_map/all_to_all | solution.py:67
  69.2 11.3 %all-to-all-start.1 = ((f32[16,1,1]{2,1,0:T(1,128)}), f32[16,1,1]{2,1,0:T(1,128)S(1)}, u32[]{:S(2)}, u32[]{:S(2)}) async-start(f32[16,1,1]{2,1,0:T(1,128)} %bitcast.29), calls=%async_computation.1 | async-start | bytes 16384 | tf_op jit(solution)/shard_map/all_to_all | solution.py:66
  80.5 11.4 %all-to-all-start.2 = ((f32[16,1,16]{2,1,0:T(1,128)}), f32[16,1,16]{2,1,0:T(1,128)S(1)}, u32[]{:S(2)}, u32[]{:S(2)}) async-start(f32[16,1,16]{2,1,0:T(1,128)} %bitcast.19), calls=%async_computation.2 | async-start | bytes 16384 | tf_op jit(solution)/shard_map/all_to_all | solution.py:65
  84.0 275.9 %all-reduce.4.cloned.1.call-start = ((), (), s32[]{:S(2)}) async-start(), calls=%async_computation.7 | async-start | bytes 196608
  108.4 260.9 %all-gather.3.cloned.1.call-start = ((), (), s32[]{:S(2)}) async-start(), calls=%async_computation.4 | async-start | bytes 5431296 | tf_op jit(solution)/shard_map/all_gather | solution.py:82
  109.2 357.3 %reduce-scatter.2.cloned.1.call-start = ((), (), s32[]{:S(2)}) async-start(), calls=%async_computation.6 | async-start | bytes 2228224 | tf_op jit(solution)/shard_map/reduce_scatter | solution.py:110
  352.8 6.4 %copy-start.2 = (f32[1,16,16]{2,1,0:T(8,128)S(1)}, f32[1,16,16]{2,1,0:T(8,128)}, u32[]{:S(2)}) copy-start(f32[1,16,16]{2,1,0:T(8,128)} %param.15) | copy-start | bytes 3076
Sparse Core Ops, SparseCore 0:
  10.4 93.2 all-gather.4
  108.6 165.0 all-reduce.3
  276.0 93.2 all-gather.2
  372.8 93.5 reduce-scatter.1
where the time goes:
time: 474 us; the launch traced here: 473 us
  blocking collectives  287 us (61%)
  waiting for transfers between devices  126 us (27%)
  matrix products  22.5 us (5%)
  starting transfers between devices  17 us (4%)
  between operations  14.5 us (3%)
    psum x1, blocking collectives, on_device(): backward_lowrank = lax.psum(back_part, 'fsdp').astype(jnp.bfloat16)  243 us
    reduce_scatter x1, waiting for transfers between devices, on_device(): lax.psum_scatter(gradient_down_partial, 'group', scatter_dimension=0, til...  90.9 us
    psum x1, blocking collectives, on_device(): lax.psum(prompt_sums(reward_row, onehot), 'group')  43.6 us
    all_gather x1, waiting for transfers between devices, on_device(): full_adapter = lax.all_gather(adapter_a, 'group', axis=0, tiled=True)  10.5 us
    all_to_all x1, starting transfers between devices, on_device(): lax.all_to_all(send_len, 'group', split_axis=0, concat_axis=0, tiled=True)  9.83 us
  transfers between devices with their start and end apart: 7, of which 5 were waited for; matrix products, arithmetic and copies ran while one was open for 5% of the time, Pallas kernels for 0%

commit v1 on v0

v1 whole, which is shorter than its diff:
```python
import jax
import jax.numpy as jnp
from jax import lax
from jax.experimental import pallas as pl
from jax.experimental.pallas import tpu as pltpu
from jax.sharding import PartitionSpec as P

COMP = 16
ADAPTER_SCALING = 0.25
SPREAD_FLOOR = 0.16

N = 16
SIDE = 4
M = 16
TOP = 3
MESH = pl.DeviceIdType.MESH
ROWS = 320
HALF = 160
F32 = jnp.float32
BF16 = jnp.bfloat16


def dot_nn(a, b):
    return lax.dot_general(a, b, (((1,), (0,)), ((), ())), preferred_element_type=F32)


def dot_nt(a, b):
    return lax.dot_general(a, b, (((1,), (1,)), ((), ())), preferred_element_type=F32)


def kernel(
    x_hbm, w_ref, a_ref, up_ref, ups_ref, new_ref, old_ref, rew_ref, len_ref, asg_ref,
    proj_ref, gdown_ref, gup_ref, loss_ref,
    xv, wg, acc, up_p, upt, og, row, tab, hs, hr, ag_a, red, rs, zx, ag, gus, gur, gds, gdr, gda,
    x_sem, h_s, h_r, a_s, a_r, zs, xs, fs, w_r, r_s, r_r, z_s, z_r, g_s, g_r, u_s, u_r, d_s, d_r, e_s, e_r,
):
    g = lax.axis_index("group")
    f = lax.axis_index("fsdp")
    z, x = lax.div(g, SIDE), lax.rem(g, SIDE)
    zh, i = lax.div(f, M), lax.rem(f, M)
    a, b = lax.div(i, SIDE), lax.rem(i, SIDE)
    hidden = w_ref.shape[0]
    cols = w_ref.shape[1]

    def copy(src, dst, ss, rr, tg, tf):
        return pltpu.make_async_remote_copy(
            src_ref=src, dst_ref=dst, send_sem=ss, recv_sem=rr,
            device_id=(tg, tf), device_id_type=MESH,
        )

    def each(fn, count=N):
        def body(d, carry):
            fn(d)
            return carry

        lax.fori_loop(1, count, body, 0)

    def group_to(d):
        return lax.rem(g + d, N)

    def group_from(d):
        return lax.rem(g + N - d, N)

    def side_to(d):
        return lax.rem(i + d, M)

    def side_from(d):
        return lax.rem(i + M - d, M)

    def top_to(d):
        return lax.rem(zh + d, TOP)

    def top_from(d):
        return lax.rem(zh + TOP - d, TOP)

    def gx(src, dst, ss, rr, d):
        return copy(src.at[group_to(d)], dst.at[g], ss.at[d], rr.at[d], group_to(d), f)

    def gx_in(src, dst, ss, rr, d):
        j = group_from(d)
        return copy(src.at[j], dst.at[j], ss.at[d], rr.at[d], j, f)

    def sx(src, dst, ss, rr, d):
        return copy(src.at[side_to(d)], dst.at[i], ss.at[d], rr.at[d], g, zh * M + side_to(d))

    def sx_in(src, dst, ss, rr, d):
        j = side_from(d)
        return copy(src.at[j], dst.at[j], ss.at[d], rr.at[d], g, zh * M + j)

    def sg(buf, ss, rr, d):
        return copy(buf.at[i], buf.at[i], ss.at[d], rr.at[d], g, zh * M + side_to(d))

    def sg_in(buf, ss, rr, d):
        j = side_from(d)
        return copy(buf.at[j], buf.at[j], ss.at[d], rr.at[d], g, zh * M + j)

    def tx(d):
        return copy(zx.at[zh], zx.at[zh], z_s.at[d], z_r.at[d], g, top_to(d) * M + i)

    def tx_in(d):
        j = top_from(d)
        return copy(zx.at[j], zx.at[j], z_s.at[d], z_r.at[d], g, j * M + i)

    x_copy = pltpu.make_async_copy(x_hbm, xv, x_sem)
    x_copy.start()

    barrier = pltpu.get_barrier_semaphore()

    def greet(d):
        pl.semaphore_signal(barrier, inc=1, device_id=(group_to(d), f), device_id_type=MESH)
        pl.semaphore_signal(barrier, inc=1, device_id=(g, zh * M + side_to(d)), device_id_type=MESH)

    each(greet)
    each(
        lambda d: pl.semaphore_signal(
            barrier, inc=1, device_id=(g, top_to(d) * M + i), device_id_type=MESH
        ),
        TOP,
    )

    wg[g, HALF + 144 : ROWS, :] = jnp.zeros((16, cols), BF16)
    wg[g, 0:hidden, :] = w_ref[...]

    rewards = rew_ref[...]
    mean = jnp.sum(rewards, axis=1, keepdims=True) / COMP
    var = jnp.sum(rewards * rewards, axis=1, keepdims=True) / COMP - mean * mean
    spread = jnp.sqrt(jnp.maximum(var, SPREAD_FLOOR))
    advantage = (rewards - mean) / spread
    dest = asg_ref[...] == lax.broadcasted_iota(jnp.int32, (N, N), 0)
    lengths = len_ref[...].astype(F32)
    old = old_ref[0]
    sent_old = jnp.zeros((N, N), F32)
    for k in range(N):
        sent_old = jnp.where(dest[:, k : k + 1], old[k : k + 1, :], sent_old)
    sent_adv = jnp.sum(jnp.where(dest, advantage, 0.0), axis=1, keepdims=True)
    sent_len = jnp.sum(jnp.where(dest, lengths, 0.0), axis=1, keepdims=True)
    hs[...] = jnp.zeros(hs.shape, F32)
    for at, value in enumerate((sent_old, sent_adv, sent_len)):
        tab[...] = jnp.zeros(tab.shape, F32)
        tab[:, 0:N] = jnp.broadcast_to(value, (N, N))
        rolled = pltpu.roll(tab[...], g * N, axis=1)
        for t in range(N):
            hs[t, at : at + 1, :] = rolled[t : t + 1, :]
    hr[g] = hs[g]
    for j in range(N):
        row[0:1, j * N : (j + 1) * N] = new_ref[0, j : j + 1, :]

    up_p[...] = jnp.zeros(up_p.shape, BF16)
    up_p[:, 0:hidden] = up_ref[...]
    upt[...] = up_p[...].astype(F32).T.astype(BF16)
    og[...] = jnp.zeros(og.shape, BF16)

    pl.semaphore_wait(barrier, 2 * (N - 1) + TOP - 1)

    each(lambda d: gx(hs, hr, h_s, h_r, d).start())

    quarter = pl.ds(pl.multiple_of(b * 128, 128), 128)

    def ax(d):
        return copy(
            a_ref.at[:, quarter], ag_a.at[z], a_s.at[d], a_r.at[z], group_to(d), f
        )

    @pl.when(x == a)
    def _():
        ag_a[z] = a_ref[:, quarter]
        each(lambda d: ax(d).start())

    right = z * SIDE + lax.rem(x + 1, SIDE)
    left = z * SIDE + lax.rem(x + SIDE - 1, SIDE)

    def part(s, h):
        return wg.at[s, pl.ds(h * HALF, HALF), :]

    def wx(s, h, sem, tg):
        return copy(part(s, h), part(s, h), sem, w_r.at[s, h], tg, f)

    def arrive(s, h):
        wx(s, h, fs.at[0, 0], g).wait_recv()

    near = [z, z + 1 - 2 * lax.rem(z, 2), 2 - lax.div(z, 2), 3 - 3 * lax.div(z, 2)]
    inner = (z == 1) | (z == 2)
    beyond = [None, 3 - z, 3 * (z - 1), 3 * (z - 1)]

    def z_first(go):
        for h in (0, 1):

            @pl.when(z < SIDE - 1)
            def _():
                go(wx(g, h, zs.at[0, h], g + SIDE))

            @pl.when(z > 0)
            def _():
                go(wx(g, h, zs.at[4, h], g - SIDE))

    def z_next(k, go):
        @pl.when(inner)
        def _():
            for h in (0, 1):
                go(wx(near[k] * SIDE + x, h, zs.at[k, h], beyond[k] * SIDE + x))

    def x_send(k, go):
        s = near[k] * SIDE + x
        go(wx(s, 0, xs.at[k, 0, 0], right))
        go(wx(s, 1, xs.at[k, 1, 1], left))
        go(wx(s, 1, xs.at[k, 0, 1], right))
        go(wx(s, 0, xs.at[k, 1, 0], left))

    def shard(k, off):
        return near[k] * SIDE + lax.rem(x + off, SIDE)

    def x_pass(k, go):
        go(wx(shard(k, 3), 0, fs.at[k, 0], right))
        go(wx(shard(k, 1), 1, fs.at[k, 1], left))

    def start(c):
        c.start()

    def done(c):
        c.wait_send()

    def pass_on(k):
        arrive(shard(k, 3), 0)
        arrive(shard(k, 1), 1)
        x_pass(k, start)

    def take(k):
        s = near[k] * SIDE + x
        arrive(s, 0)
        arrive(s, 1)
        z_next(k, start)

    def multiply(s, first=False):
        piece = dot_nt(wg[s], xv[:, pl.ds(pl.multiple_of(s * cols, cols), cols)])
        if first:
            acc[...] = piece
        else:
            acc[...] += piece

    def finish(k):
        arrive(shard(k, 3), 1)
        multiply(shard(k, 3))
        arrive(shard(k, 1), 0)
        multiply(shard(k, 1))
        arrive(shard(k, 2), 0)
        arrive(shard(k, 2), 1)
        multiply(shard(k, 2))

    z_first(start)
    x_send(0, start)

    each(lambda d: gx_in(hs, hr, h_s, h_r, d).wait_recv())
    got = hr[0]
    for j in range(1, N):
        got = got + hr[j]
    recv_old, recv_adv, recv_len = got[0:1, :], got[1:2, :], got[2:3, :]
    position = lax.rem(lax.broadcasted_iota(jnp.int32, (1, N * N), 1), N).astype(F32)
    ratio = jnp.exp(row[0:1, :] - recv_old)
    coef = jnp.where(position < recv_len, -(recv_adv * ratio) / (recv_len * COMP), 0.0)
    loss_ref[...] = jnp.sum(coef, axis=1, keepdims=True)
    og[0:hidden, :] = (coef * ups_ref[...].astype(F32)).astype(BF16)
    back = dot_nn(up_p[...], og[...])
    for p in range(8):
        red[8 + p] = back[p * 8 : (p + 1) * 8, :]

    pass_on(0)

    for q in range(SIDE):

        @pl.when((x != a) | (z != q))
        def _():
            copy(
                a_ref.at[:, quarter], ag_a.at[q], a_s.at[0], a_r.at[q], g, f
            ).wait_recv()

    x_copy.wait()
    low = jnp.zeros((64, N * N), F32)
    for q in range(SIDE):
        at = (q * SIDE + a) * cols + b * 128
        low = low + dot_nt(ag_a[q], xv[:, pl.ds(pl.multiple_of(at, 128), 128)])
    for p in range(8):
        red[p] = low[p * 8 : (p + 1) * 8, :]
    rs[i] = red[i]
    each(lambda d: sx(red, rs, r_s, r_r, d).start())

    take(1)
    x_send(1, start)
    take(2)
    x_send(2, start)
    multiply(g, first=True)

    each(lambda d: sx_in(red, rs, r_s, r_r, d).wait_recv())
    total = rs[0]
    for j in range(1, M):
        total = total + rs[j]
    ag[i] = total.astype(BF16).astype(F32)

    @pl.when(i >= 8)
    def _():
        zx[zh] = total
        each(lambda d: tx(d).start(), TOP)

    pass_on(1)
    take(3)

    @pl.when(i >= 8)
    def _():
        each(lambda d: tx_in(d).wait_recv(), TOP)
        ag[i] = (zx[0] + zx[1] + zx[2]).astype(BF16).astype(F32)

    each(lambda d: sg(ag, g_s, g_r, d).start())

    finish(0)
    multiply(shard(1, 0))
    pass_on(2)

    each(lambda d: sg_in(ag, g_s, g_r, d).wait_recv())
    low_b = ag[0:8].reshape(64, N * N).astype(BF16)
    gp = ADAPTER_SCALING * dot_nt(low_b, og[...])
    for t in range(N):
        gus[t] = gp[t * 4 : (t + 1) * 4, :]
    gur[g] = gus[g]
    each(lambda d: gx(gus, gur, u_s, u_r, d).start())
    bl = ag[8 + lax.div(i, 2)].astype(BF16)
    low_half = lax.rem(i, 2) == 0

    def down(t, carry):
        full = ADAPTER_SCALING * dot_nn(bl, xv[:, pl.ds(pl.multiple_of(t * cols, cols), cols)])
        gds[t] = jnp.where(low_half, full[0:4, :], full[4:8, :])
        return carry

    lax.fori_loop(0, N, down, 0)
    gdr[g] = gds[g]
    each(lambda d: gx(gds, gdr, d_s, d_r, d).start())

    x_send(3, start)

    finish(1)
    multiply(shard(2, 0))
    finish(2)
    multiply(shard(3, 0))

    each(lambda d: gx_in(gus, gur, u_s, u_r, d).wait_recv())
    total_up = gur[0]
    for j in range(1, N):
        total_up = total_up + gur[j]
    gup_ref[...] = total_up[:, 0:hidden]
    each(lambda d: gx_in(gds, gdr, d_s, d_r, d).wait_recv())
    total_down = gdr[0]
    for j in range(1, N):
        total_down = total_down + gdr[j]
    gda[i] = total_down
    each(lambda d: sg(gda, e_s, e_r, d).start())

    pass_on(3)
    acc[...] += ADAPTER_SCALING * dot_nn(upt[0:ROWS, :], low_b)
    finish(3)
    proj_ref[...] = acc[0:hidden, :].astype(BF16)

    each(lambda d: sg_in(gda, e_s, e_r, d).wait_recv())
    for j in range(M):
        gdown_ref[j * 4 : (j + 1) * 4, :] = gda[j]

    each(lambda d: gx(hs, hr, h_s, h_r, d).wait_send())

    @pl.when(x == a)
    def _():
        each(lambda d: ax(d).wait_send())

    z_first(done)
    for k in range(1, SIDE):
        z_next(k, done)
    for k in range(SIDE):
        x_send(k, done)
        x_pass(k, done)
    each(lambda d: sx(red, rs, r_s, r_r, d).wait_send())

    @pl.when(i >= 8)
    def _():
        each(lambda d: tx(d).wait_send(), TOP)

    each(lambda d: sg(ag, g_s, g_r, d).wait_send())
    each(lambda d: gx(gus, gur, u_s, u_r, d).wait_send())
    each(lambda d: gx(gds, gdr, d_s, d_r, d).wait_send())
    each(lambda d: sg(gda, e_s, e_r, d).wait_send())


def on_device(
    hidden_input_slots,
    base_weight,
    adapter_a,
    adapter_up_matrix,
    upstream,
    logp_new,
    logp_old,
    rewards,
    comp_lengths,
    assignment,
):
    tokens, depth = hidden_input_slots.shape
    share, hidden = base_weight.shape
    rank = adapter_a.shape[1]
    vmem = pl.BlockSpec(memory_space=pltpu.VMEM)
    dma = pltpu.SemaphoreType.DMA
    projection, down, up, loss = pl.pallas_call(
        kernel,
        out_shape=(
            jax.ShapeDtypeStruct((hidden, tokens), BF16),
            jax.ShapeDtypeStruct((rank, share), F32),
            jax.ShapeDtypeStruct((rank // N, hidden), F32),
            jax.ShapeDtypeStruct((1, 1), F32),
        ),
        in_specs=[pl.BlockSpec(memory_space=pl.ANY)] + [vmem] * 9,
        out_specs=(vmem,) * 4,
        scratch_shapes=[
            pltpu.VMEM((tokens, depth), BF16),
            pltpu.VMEM((N, ROWS, share), BF16),
            pltpu.VMEM((ROWS, tokens), F32),
            pltpu.VMEM((rank, 384), BF16),
            pltpu.VMEM((384, rank), BF16),
            pltpu.VMEM((384, tokens), BF16),
            pltpu.VMEM((8, tokens), F32),
            pltpu.VMEM((N, tokens), F32),
            pltpu.VMEM((N, 8, tokens), F32),
            pltpu.VMEM((N, 8, tokens), F32),
            pltpu.VMEM((SIDE, rank, 128), BF16),
            pltpu.VMEM((M, 8, tokens), F32),
            pltpu.VMEM((M, 8, tokens), F32),
            pltpu.VMEM((TOP, 8, tokens), F32),
            pltpu.VMEM((M, 8, tokens), F32),
            pltpu.VMEM((N, 4, 384), F32),
            pltpu.VMEM((N, 4, 384), F32),
            pltpu.VMEM((N, 4, share), F32),
            pltpu.VMEM((N, 4, share), F32),
            pltpu.VMEM((M, 4, share), F32),
            dma,
            dma((N,)), dma((N,)),
            dma((N,)), dma((SIDE,)),
            dma((5, 2)), dma((SIDE, 2, 2)), dma((SIDE, 2)), dma((N, 2)),
            dma((M,)), dma((M,)),
            dma((TOP,)), dma((TOP,)),
            dma((M,)), dma((M,)),
            dma((N,)), dma((N,)),
            dma((N,)), dma((N,)),
            dma((M,)), dma((M,)),
        ],
        compiler_params=pltpu.CompilerParams(collective_id=0, has_side_effects=True),
    )(
        hidden_input_slots,
        base_weight.T,
        adapter_a.T,
        adapter_up_matrix,
        upstream.T,
        logp_new,
        logp_old,
        rewards,
        comp_lengths,
        assignment,
    )
    return (projection.T, down.T, up, loss.reshape(1))


def solution(mesh):
    return jax.shard_map(
        on_device,
        mesh=mesh,
        in_specs=(
            P("group", None),
            P("group", "fsdp"),
            P("group", None),
            P(None, "fsdp"),
            P("group", "fsdp"),
            P("group", None, None),
            P("group", None, None),
            P("group", None),
            P("group", None),
            P("group", None),
        ),
        out_specs=(P("group", "fsdp"), P("group", None), P("group", "fsdp"), P("group")),
        check_vma=False,
    )
```

time: 474 us -> 85 us (0.18)
  the two profiles are of different devices: /device:TPU:8 before, /device:TPU:1 now
where the time goes in v1:
time: 85 us; the launch traced here: 83.4 us
  Pallas kernels  76.5 us (90%)
  local copies, waits for them, and re-layouts  4.44 us (5%)
  between operations  2.46 us (3%)
    pallas_call x1, Pallas kernels, on_device(): pl.pallas_call(kernel, out_shape=(jax.ShapeDtypeStruct((hidden, tokens),...  76.5 us
    unnamed x3, local copies, waits for them, and re-layouts  4.44 us

profile of v1, /device:TPU:1, one launch (start us, length us, event | category | flops | bytes accessed | tf_op | source)
XLA Modules:
  0.0 83.4 jit_solution(15334552020851906318)
XLA Ops:
  0.6 76.5 %shard_map.129 = (bf16[308,256]{1,0:T(8,128)(2,1)}, f32[64,512]{1,0:T(8,128)}, f32[4,308]{1,0:T(4,128)}, f32[1,1]{1,0:T(1,128)}) custom-call(bf16[256,8192]{1,0:T(8,128)(2,1)} %x_hbm.1, bf16[308,512]{1,0:T(8,128)(2,1)} %bitcast.6, bf16[64,512]{1,0:T(8,128)(2,1)} %bitcast.10, bf16[64,308]{1,0:T(8,128)(2,1)} %up_ref.1, bf16[308,256]{1,0:T(8,128)(2,1)} %bitcast.7, ...), custom_call_target="tpu_custom_call" | custom-call | tf_op jit(solution)/shard_map/pallas_call | solution.py:405
  77.1 1.6 %copy.18 = bf16[256,308]{0,1:T(8,128)(2,1)} copy(bf16[256,308]{0,1:T(8,128)(2,1)} %bitcast.8) | data formatting | bytes 315392
  78.7 1.6 %copy.19 = f32[512,64]{0,1:T(8,128)} copy(f32[512,64]{0,1:T(8,128)} %bitcast.9) | data formatting | bytes 262144
  80.3 1.3 %copy.20 = f32[4,308]{1,0:T(4,128)} copy(f32[4,308]{1,0:T(4,128)} %get-tuple-element.18) | data formatting | bytes 9856

commit v2 on v1

--- a/solution.py
+++ b/solution.py
@@ -15,7 +15,9 @@
 TOP = 3
 MESH = pl.DeviceIdType.MESH
 ROWS = 320
-HALF = 160
+SPLIT = 256
+HALF = SPLIT // 2
+REST = ROWS - SPLIT
 F32 = jnp.float32
 BF16 = jnp.bfloat16
 
@@ -31,8 +33,8 @@
 def kernel(
     x_hbm, w_ref, a_ref, up_ref, ups_ref, new_ref, old_ref, rew_ref, len_ref, asg_ref,
     proj_ref, gdown_ref, gup_ref, loss_ref,
-    xv, wg, acc, up_p, upt, og, row, tab, hs, hr, ag_a, red, rs, zx, ag, gus, gur, gds, gdr, gda,
-    x_sem, h_s, h_r, a_s, a_r, zs, xs, fs, w_r, r_s, r_r, z_s, z_r, g_s, g_r, u_s, u_r, d_s, d_r, e_s, e_r,
+    xv, wg, acc, up_p, upt, og, row, tab, hs, hr, ag_a, red, rs, zx, ag, lows, gus, gur, gds, gdr, gda,
+    x_sem, h_s, h_r, a_s, a_r, zs, xs, fs, w_r, qx_s, qx_r, qz_s, qz_r, r_s, r_r, z_s, z_r, g_s, g_r, u_s, u_r, d_s, d_r, e_s, e_r,
 ):
     g = lax.axis_index("group")
     f = lax.axis_index("fsdp")
@@ -118,7 +120,7 @@
         TOP,
     )
 
-    wg[g, HALF + 144 : ROWS, :] = jnp.zeros((16, cols), BF16)
+    wg[g, ROWS - 16 : ROWS, :] = jnp.zeros((16, cols), BF16)
     wg[g, 0:hidden, :] = w_ref[...]
 
     rewards = rew_ref[...]
@@ -194,10 +196,8 @@
                 go(wx(g, h, zs.at[4, h], g - SIDE))
 
     def z_next(k, go):
-        @pl.when(inner)
-        def _():
-            for h in (0, 1):
-                go(wx(near[k] * SIDE + x, h, zs.at[k, h], beyond[k] * SIDE + x))
+        for h in (0, 1):
+            go(wx(near[k] * SIDE + x, h, zs.at[k, h], beyond[k] * SIDE + x))
 
     def x_send(k, go):
         s = near[k] * SIDE + x
@@ -224,18 +224,71 @@
         arrive(shard(k, 1), 1)
         x_pass(k, start)
 
-    def take(k):
-        s = near[k] * SIDE + x
-        arrive(s, 0)
-        arrive(s, 1)
-        z_next(k, start)
+    def land(k):
+        arrive(near[k] * SIDE + x, 0)
+        arrive(near[k] * SIDE + x, 1)
+
+    def q_copy(ref, sem, rem, tg):
+        return copy(ref, ref, sem, rem, tg, f)
+
+    def q_part(s):
+        return wg.at[s, pl.ds(SPLIT, REST), :]
+
+    def q_half(s, h):
+        return wg.at[s, pl.ds(SPLIT + h * (REST // 2), REST // 2), :]
+
+    def q_rows(zz):
+        return wg.at[pl.ds(zz * SIDE, SIDE), pl.ds(SPLIT, REST), :]
+
+    def q_send(go):
+        go(q_copy(q_part(g), qx_s.at[0], qx_r.at[0], right))
+        go(q_copy(q_part(g), qx_s.at[1], qx_r.at[1], left))
+
+    def q_pass(go):
+        go(q_copy(q_half(shard(0, 3), 0), qx_s.at[2], qx_r.at[2], right))
+        go(q_copy(q_half(shard(0, 1), 1), qx_s.at[3], qx_r.at[3], left))
+
+    def q_first(go):
+        @pl.when(z < SIDE - 1)
+        def _():
+            go(q_copy(q_rows(z), qz_s.at[0], qz_r.at[z], g + SIDE))
+
+        @pl.when(z > 0)
+        def _():
+            go(q_copy(q_rows(z), qz_s.at[4], qz_r.at[z], g - SIDE))
+
+    def q_next(k, go):
+        go(q_copy(q_rows(near[k]), qz_s.at[k], qz_r.at[near[k]], beyond[k] * SIDE + x))
+
+    def q_land(k):
+        q_copy(q_rows(near[k]), qz_s.at[0], qz_r.at[near[k]], g).wait_recv()
+
+    def q_relay(k):
+        @pl.when(inner)
+        def _():
+            q_land(k)
+            q_next(k, start)
+
+    def x_block(s):
+        return xv[:, pl.ds(pl.multiple_of(s * cols, cols), cols)]
 
     def multiply(s, first=False):
-        piece = dot_nt(wg[s], xv[:, pl.ds(pl.multiple_of(s * cols, cols), cols)])
+        piece = dot_nt(wg[s, 0:SPLIT, :], x_block(s))
         if first:
-            acc[...] = piece
+            acc[0:SPLIT, :] = piece
         else:
-            acc[...] += piece
+            acc[0:SPLIT, :] += piece
+
+    def q_multiply(k, first=False):
+        piece = None
+        for off in range(SIDE):
+            s = near[k] * SIDE + off
+            term = dot_nt(wg[s, SPLIT:ROWS, :], x_block(s))
+            piece = term if piece is None else piece + term
+        if first:
+            acc[SPLIT:ROWS, :] = piece
+        else:
+            acc[SPLIT:ROWS, :] += piece
 
     def finish(k):
         arrive(shard(k, 3), 1)
@@ -246,6 +299,7 @@
         arrive(shard(k, 2), 1)
         multiply(shard(k, 2))
 
+    q_send(start)
     z_first(start)
     x_send(0, start)
 
@@ -260,10 +314,12 @@
     loss_ref[...] = jnp.sum(coef, axis=1, keepdims=True)
     og[0:hidden, :] = (coef * ups_ref[...].astype(F32)).astype(BF16)
     back = dot_nn(up_p[...], og[...])
-    for p in range(8):
-        red[8 + p] = back[p * 8 : (p + 1) * 8, :]
-
-    pass_on(0)
+    for p in range(M):
+        red[p, 4:8, :] = back[p * 4 : (p + 1) * 4, :]
+
+    q_copy(q_part(shard(0, 3)), qx_s.at[0], qx_r.at[0], g).wait_recv()
+    q_copy(q_part(shard(0, 1)), qx_s.at[0], qx_r.at[1], g).wait_recv()
+    q_pass(start)
 
     for q in range(SIDE):
 
@@ -278,73 +334,87 @@
     for q in range(SIDE):
         at = (q * SIDE + a) * cols + b * 128
         low = low + dot_nt(ag_a[q], xv[:, pl.ds(pl.multiple_of(at, 128), 128)])
-    for p in range(8):
-        red[p] = low[p * 8 : (p + 1) * 8, :]
+    for p in range(M):
+        red[p, 0:4, :] = low[p * 4 : (p + 1) * 4, :]
     rs[i] = red[i]
     each(lambda d: sx(red, rs, r_s, r_r, d).start())
 
-    take(1)
+    pass_on(0)
+    land(1)
+
+    @pl.when(inner)
+    def _():
+        z_next(1, start)
+
     x_send(1, start)
-    take(2)
-    x_send(2, start)
+
+    @pl.when(inner)
+    def _():
+        land(2)
+        z_next(2, start)
+
+    q_copy(q_half(shard(0, 2), 0), qx_s.at[0], qx_r.at[2], g).wait_recv()
+    q_copy(q_half(shard(0, 2), 1), qx_s.at[0], qx_r.at[3], g).wait_recv()
+    q_first(start)
     multiply(g, first=True)
 
     each(lambda d: sx_in(red, rs, r_s, r_r, d).wait_recv())
     total = rs[0]
     for j in range(1, M):
         total = total + rs[j]
-    ag[i] = total.astype(BF16).astype(F32)
-
-    @pl.when(i >= 8)
-    def _():
-        zx[zh] = total
-        each(lambda d: tx(d).start(), TOP)
+    zx[zh] = total
+    each(lambda d: tx(d).start(), TOP)
+    ag[i] = total[0:4, :].astype(BF16).astype(F32)
+    each(lambda d: sg(ag, g_s, g_r, d).start())
+
+    @pl.when(inner)
+    def _():
+        land(3)
+        z_next(3, start)
 
     pass_on(1)
-    take(3)
-
-    @pl.when(i >= 8)
-    def _():
-        each(lambda d: tx_in(d).wait_recv(), TOP)
-        ag[i] = (zx[0] + zx[1] + zx[2]).astype(BF16).astype(F32)
-
-    each(lambda d: sg(ag, g_s, g_r, d).start())
-
+    q_relay(1)
+
+    each(lambda d: tx_in(d).wait_recv(), TOP)
+    bl = (zx[0] + zx[1] + zx[2]).astype(BF16)
+
+    def down(t, carry):
+        full = ADAPTER_SCALING * dot_nn(bl, x_block(t))
+        gds[t] = full[4:8, :]
+        return carry
+
+    lax.fori_loop(0, N, down, 0)
+    gdr[g] = gds[g]
+    each(lambda d: gx(gds, gdr, d_s, d_r, d).start())
+
+    @pl.when(jnp.logical_not(inner))
+    def _():
+        land(2)
+
+    x_send(2, start)
+    q_relay(2)
     finish(0)
     multiply(shard(1, 0))
-    pass_on(2)
 
     each(lambda d: sg_in(ag, g_s, g_r, d).wait_recv())
-    low_b = ag[0:8].reshape(64, N * N).astype(BF16)
+    for j in range(M):
+        lows[j * 4 : (j + 1) * 4, :] = ag[j]
+    low_b = lows[...].astype(BF16)
     gp = ADAPTER_SCALING * dot_nt(low_b, og[...])
     for t in range(N):
         gus[t] = gp[t * 4 : (t + 1) * 4, :]
     gur[g] = gus[g]
     each(lambda d: gx(gus, gur, u_s, u_r, d).start())
-    bl = ag[8 + lax.div(i, 2)].astype(BF16)
-    low_half = lax.rem(i, 2) == 0
-
-    def down(t, carry):
-        full = ADAPTER_SCALING * dot_nn(bl, xv[:, pl.ds(pl.multiple_of(t * cols, cols), cols)])
-        gds[t] = jnp.where(low_half, full[0:4, :], full[4:8, :])
-        return carry
-
-    lax.fori_loop(0, N, down, 0)
-    gdr[g] = gds[g]
-    each(lambda d: gx(gds, gdr, d_s, d_r, d).start())
+
+    pass_on(2)
+
+    @pl.when(jnp.logical_not(inner))
+    def _():
+        land(3)
 
     x_send(3, start)
-
-    finish(1)
-    multiply(shard(2, 0))
-    finish(2)
-    multiply(shard(3, 0))
-
-    each(lambda d: gx_in(gus, gur, u_s, u_r, d).wait_recv())
-    total_up = gur[0]
-    for j in range(1, N):
-        total_up = total_up + gur[j]
-    gup_ref[...] = total_up[:, 0:hidden]
+    q_relay(3)
+
     each(lambda d: gx_in(gds, gdr, d_s, d_r, d).wait_recv())
     total_down = gdr[0]
     for j in range(1, N):
@@ -352,14 +422,38 @@
     gda[i] = total_down
     each(lambda d: sg(gda, e_s, e_r, d).start())
 
+    q_multiply(0, first=True)
+    finish(1)
+    multiply(shard(2, 0))
+    acc[...] += ADAPTER_SCALING * dot_nn(upt[0:ROWS, :], low_b)
+    each(lambda d: gx_in(gus, gur, u_s, u_r, d).wait_recv())
+    total_up = gur[0]
+    for j in range(1, N):
+        total_up = total_up + gur[j]
+    gup_ref[...] = total_up[:, 0:hidden]
+
     pass_on(3)
-    acc[...] += ADAPTER_SCALING * dot_nn(upt[0:ROWS, :], low_b)
-    finish(3)
-    proj_ref[...] = acc[0:hidden, :].astype(BF16)
-
+    multiply(shard(3, 0))
     each(lambda d: sg_in(gda, e_s, e_r, d).wait_recv())
     for j in range(M):
         gdown_ref[j * 4 : (j + 1) * 4, :] = gda[j]
+    finish(2)
+    for k in (1, 2):
+
+        @pl.when(jnp.logical_not(inner))
+        def _():
+            q_land(k)
+
+        q_multiply(k)
+
+    finish(3)
+
+    @pl.when(jnp.logical_not(inner))
+    def _():
+        q_land(3)
+
+    q_multiply(3)
+    proj_ref[...] = acc[0:hidden, :].astype(BF16)
 
     each(lambda d: gx(hs, hr, h_s, h_r, d).wait_send())
 
@@ -367,18 +461,22 @@
     def _():
         each(lambda d: ax(d).wait_send())
 
+    q_send(done)
+    q_pass(done)
+    q_first(done)
     z_first(done)
-    for k in range(1, SIDE):
-        z_next(k, done)
+
+    @pl.when(inner)
+    def _():
+        for k in range(1, SIDE):
+            z_next(k, done)
+            q_next(k, done)
+
     for k in range(SIDE):
         x_send(k, done)
         x_pass(k, done)
     each(lambda d: sx(red, rs, r_s, r_r, d).wait_send())
-
-    @pl.when(i >= 8)
-    def _():
-        each(lambda d: tx(d).wait_send(), TOP)
-
+    each(lambda d: tx(d).wait_send(), TOP)
     each(lambda d: sg(ag, g_s, g_r, d).wait_send())
     each(lambda d: gx(gus, gur, u_s, u_r, d).wait_send())
     each(lambda d: gx(gds, gdr, d_s, d_r, d).wait_send())
@@ -427,7 +525,8 @@
             pltpu.VMEM((M, 8, tokens), F32),
             pltpu.VMEM((M, 8, tokens), F32),
             pltpu.VMEM((TOP, 8, tokens), F32),
-            pltpu.VMEM((M, 8, tokens), F32),
+            pltpu.VMEM((M, 4, tokens), F32),
+            pltpu.VMEM((rank, tokens), F32),
             pltpu.VMEM((N, 4, 384), F32),
             pltpu.VMEM((N, 4, 384), F32),
             pltpu.VMEM((N, 4, share), F32),
@@ -437,6 +536,7 @@
             dma((N,)), dma((N,)),
             dma((N,)), dma((SIDE,)),
             dma((5, 2)), dma((SIDE, 2, 2)), dma((SIDE, 2)), dma((N, 2)),
+            dma((4,)), dma((4,)), dma((5,)), dma((SIDE,)),
             dma((M,)), dma((M,)),
             dma((TOP,)), dma((TOP,)),
             dma((M,)), dma((M,)),

time: 85 us -> 83.4 us (0.981)
  the two profiles are of different devices: /device:TPU:1 before, /device:TPU:64 now
where the time goes in v2:
time: 83.4 us; the launch traced here: 83.2 us
  Pallas kernels  76.3 us (91%)
  local copies, waits for them, and re-layouts  4.44 us (5%)
  between operations  2.46 us (3%)
    pallas_call x1, Pallas kernels, on_device(): pl.pallas_call(kernel, out_shape=(jax.ShapeDtypeStruct((hidden, tokens),...  76.3 us
    unnamed x3, local copies, waits for them, and re-layouts  4.44 us

profile of v2, /device:TPU:64, one launch (start us, length us, event | category | flops | bytes accessed | tf_op | source)
XLA Modules:
  0.0 83.2 jit_solution(256274665597856740)
XLA Ops:
  0.6 76.3 %shard_map.129 = (bf16[308,256]{1,0:T(8,128)(2,1)}, f32[64,512]{1,0:T(8,128)}, f32[4,308]{1,0:T(4,128)}, f32[1,1]{1,0:T(1,128)}) custom-call(bf16[256,8192]{1,0:T(8,128)(2,1)} %x_hbm.1, bf16[308,512]{1,0:T(8,128)(2,1)} %bitcast.6, bf16[64,512]{1,0:T(8,128)(2,1)} %bitcast.10, bf16[64,308]{1,0:T(8,128)(2,1)} %up_ref.1, bf16[308,256]{1,0:T(8,128)(2,1)} %bitcast.7, ...), custom_call_target="tpu_custom_call" | custom-call | tf_op jit(solution)/shard_map/pallas_call | solution.py:503
  76.9 1.6 %copy.18 = bf16[256,308]{0,1:T(8,128)(2,1)} copy(bf16[256,308]{0,1:T(8,128)(2,1)} %bitcast.8) | data formatting | bytes 315392
  78.5 1.6 %copy.19 = f32[512,64]{0,1:T(8,128)} copy(f32[512,64]{0,1:T(8,128)} %bitcast.9) | data formatting | bytes 262144
  80.1 1.3 %copy.20 = f32[4,308]{1,0:T(4,128)} copy(f32[4,308]{1,0:T(4,128)} %get-tuple-element.18) | data formatting | bytes 9856

commit v3 on v2

--- a/solution.py
+++ b/solution.py
@@ -154,8 +154,6 @@
 
     pl.semaphore_wait(barrier, 2 * (N - 1) + TOP - 1)
 
-    each(lambda d: gx(hs, hr, h_s, h_r, d).start())
-
     quarter = pl.ds(pl.multiple_of(b * 128, 128), 128)
 
     def ax(d):
@@ -163,10 +161,16 @@
             a_ref.at[:, quarter], ag_a.at[z], a_s.at[d], a_r.at[z], group_to(d), f
         )
 
+    gives = (x == a) & (z - 1 + lax.div(SIDE - z, SIDE) == zh)
     @pl.when(x == a)
     def _():
         ag_a[z] = a_ref[:, quarter]
+
+    @pl.when(gives)
+    def _():
         each(lambda d: ax(d).start())
+
+    each(lambda d: gx(hs, hr, h_s, h_r, d).start())
 
     right = z * SIDE + lax.rem(x + 1, SIDE)
     left = z * SIDE + lax.rem(x + SIDE - 1, SIDE)
@@ -182,6 +186,7 @@
 
     near = [z, z + 1 - 2 * lax.rem(z, 2), 2 - lax.div(z, 2), 3 - 3 * lax.div(z, 2)]
     inner = (z == 1) | (z == 2)
+    outer = (z == 0) | (z == 3)
     beyond = [None, 3 - z, 3 * (z - 1), 3 * (z - 1)]
 
     def z_first(go):
@@ -321,19 +326,28 @@
     q_copy(q_part(shard(0, 1)), qx_s.at[0], qx_r.at[1], g).wait_recv()
     q_pass(start)
 
-    for q in range(SIDE):
-
+    def adapter(q, at_first):
         @pl.when((x != a) | (z != q))
         def _():
             copy(
                 a_ref.at[:, quarter], ag_a.at[q], a_s.at[0], a_r.at[q], g, f
             ).wait_recv()
 
+        at = (q * SIDE + a) * cols + b * 128
+        term = dot_nt(ag_a[q], xv[:, pl.ds(pl.multiple_of(at, 128), 128)])
+        if at_first:
+            lows[...] = term
+        else:
+            lows[...] += term
+
     x_copy.wait()
-    low = jnp.zeros((64, N * N), F32)
-    for q in range(SIDE):
-        at = (q * SIDE + a) * cols + b * 128
-        low = low + dot_nt(ag_a[q], xv[:, pl.ds(pl.multiple_of(at, 128), 128)])
+    adapter(zh + 1, True)
+
+    @pl.when(zh == 0)
+    def _():
+        adapter(0, False)
+
+    low = lows[...]
     for p in range(M):
         red[p, 0:4, :] = low[p * 4 : (p + 1) * 4, :]
     rs[i] = red[i]
@@ -352,10 +366,8 @@
     def _():
         land(2)
         z_next(2, start)
-
-    q_copy(q_half(shard(0, 2), 0), qx_s.at[0], qx_r.at[2], g).wait_recv()
-    q_copy(q_half(shard(0, 2), 1), qx_s.at[0], qx_r.at[3], g).wait_recv()
-    q_first(start)
+        x_send(2, start)
+
     multiply(g, first=True)
 
     each(lambda d: sx_in(red, rs, r_s, r_r, d).wait_recv())
@@ -364,34 +376,48 @@
         total = total + rs[j]
     zx[zh] = total
     each(lambda d: tx(d).start(), TOP)
-    ag[i] = total[0:4, :].astype(BF16).astype(F32)
-    each(lambda d: sg(ag, g_s, g_r, d).start())
+
+    q_copy(q_half(shard(0, 2), 0), qx_s.at[0], qx_r.at[2], g).wait_recv()
+    q_copy(q_half(shard(0, 2), 1), qx_s.at[0], qx_r.at[3], g).wait_recv()
 
     @pl.when(inner)
     def _():
         land(3)
         z_next(3, start)
 
+    q_first(start)
+
+    @pl.when(outer)
+    def _():
+        land(2)
+        x_send(2, start)
+
     pass_on(1)
-    q_relay(1)
 
     each(lambda d: tx_in(d).wait_recv(), TOP)
-    bl = (zx[0] + zx[1] + zx[2]).astype(BF16)
+    whole = zx[0] + zx[1] + zx[2]
+    ag[i] = whole[0:4, :].astype(BF16).astype(F32)
+    each(lambda d: sg(ag, g_s, g_r, d).start())
+    bl = whole.astype(BF16)
 
     def down(t, carry):
-        full = ADAPTER_SCALING * dot_nn(bl, x_block(t))
-        gds[t] = full[4:8, :]
+        for u in range(SIDE):
+            full = ADAPTER_SCALING * dot_nn(bl, x_block(t * SIDE + u))
+            gds[t * SIDE + u] = full[4:8, :]
         return carry
 
-    lax.fori_loop(0, N, down, 0)
+    lax.fori_loop(0, SIDE, down, 0)
     gdr[g] = gds[g]
     each(lambda d: gx(gds, gdr, d_s, d_r, d).start())
 
-    @pl.when(jnp.logical_not(inner))
-    def _():
-        land(2)
-
-    x_send(2, start)
+    pass_on(2)
+
+    @pl.when(outer)
+    def _():
+        land(3)
+
+    x_send(3, start)
+    q_relay(1)
     q_relay(2)
     finish(0)
     multiply(shard(1, 0))
@@ -406,14 +432,8 @@
     gur[g] = gus[g]
     each(lambda d: gx(gus, gur, u_s, u_r, d).start())
 
-    pass_on(2)
-
-    @pl.when(jnp.logical_not(inner))
-    def _():
-        land(3)
-
-    x_send(3, start)
     q_relay(3)
+    pass_on(3)
 
     each(lambda d: gx_in(gds, gdr, d_s, d_r, d).wait_recv())
     total_down = gdr[0]
@@ -423,41 +443,39 @@
     each(lambda d: sg(gda, e_s, e_r, d).start())
 
     q_multiply(0, first=True)
+    acc[...] += ADAPTER_SCALING * dot_nn(upt[0:ROWS, :], low_b)
     finish(1)
     multiply(shard(2, 0))
-    acc[...] += ADAPTER_SCALING * dot_nn(upt[0:ROWS, :], low_b)
+    finish(2)
+    multiply(shard(3, 0))
+    for k in (1, 2):
+
+        @pl.when(outer)
+        def _():
+            q_land(k)
+
+        q_multiply(k)
+
     each(lambda d: gx_in(gus, gur, u_s, u_r, d).wait_recv())
     total_up = gur[0]
     for j in range(1, N):
         total_up = total_up + gur[j]
     gup_ref[...] = total_up[:, 0:hidden]
 
-    pass_on(3)
-    multiply(shard(3, 0))
+    @pl.when(outer)
+    def _():
+        q_land(3)
+
+    q_multiply(3)
     each(lambda d: sg_in(gda, e_s, e_r, d).wait_recv())
     for j in range(M):
         gdown_ref[j * 4 : (j + 1) * 4, :] = gda[j]
-    finish(2)
-    for k in (1, 2):
-
-        @pl.when(jnp.logical_not(inner))
-        def _():
-            q_land(k)
-
-        q_multiply(k)
-
     finish(3)
-
-    @pl.when(jnp.logical_not(inner))
-    def _():
-        q_land(3)
-
-    q_multiply(3)
     proj_ref[...] = acc[0:hidden, :].astype(BF16)
 
     each(lambda d: gx(hs, hr, h_s, h_r, d).wait_send())
 
-    @pl.when(x == a)
+    @pl.when(gives)
     def _():
         each(lambda d: ax(d).wait_send())
 
@@ -481,6 +499,11 @@
     each(lambda d: gx(gus, gur, u_s, u_r, d).wait_send())
     each(lambda d: gx(gds, gdr, d_s, d_r, d).wait_send())
     each(lambda d: sg(gda, e_s, e_r, d).wait_send())
+
+
+def keep(*refs):
+    for taken, given in zip(refs[:4], refs[4:]):
+        given[...] = taken[...]
 
 
 def on_device(
@@ -557,6 +580,15 @@
         comp_lengths,
         assignment,
     )
+    kept = pl.pallas_call(
+        keep,
+        out_shape=tuple(
+            jax.ShapeDtypeStruct(v.shape, v.dtype) for v in (projection, down, up, loss)
+        ),
+        in_specs=[vmem] * 4,
+        out_specs=(vmem,) * 4,
+    )(projection, down, up, loss)
+    projection, down, up, loss = kept
     return (projection.T, down.T, up, loss.reshape(1))
 
 

time: 83.4 us -> 71.1 us (0.85)
  the two profiles are of different devices: /device:TPU:64 before, /device:TPU:1 now
where the time goes in v3:
time: 71.1 us; the launch traced here: 71 us
  Pallas kernels  70.3 us (99%)
    pallas_call x1, Pallas kernels, on_device(): pl.pallas_call(kernel, out_shape=(jax.ShapeDtypeStruct((hidden, tokens),...  68.1 us
    pallas_call x1, Pallas kernels, on_device(): pl.pallas_call(keep, out_shape=tuple((jax.ShapeDtypeStruct(v.shape, v.dty...  2.26 us

profile of v3, /device:TPU:1, one launch (start us, length us, event | category | flops | bytes accessed | tf_op | source)
XLA Modules:
  0.0 71.0 jit_solution(9097295536769629104)
XLA Ops:
  0.6 68.1 %shard_map.129 = (bf16[308,256]{1,0:T(8,128)(2,1)}, f32[64,512]{1,0:T(8,128)}, f32[4,308]{1,0:T(4,128)}, f32[1,1]{1,0:T(1,128)}) custom-call(bf16[256,8192]{1,0:T(8,128)(2,1)} %x_hbm.1, bf16[308,512]{1,0:T(8,128)(2,1)} %bitcast.6, bf16[64,512]{1,0:T(8,128)(2,1)} %bitcast.8, bf16[64,308]{1,0:T(8,128)(2,1)} %up_ref.1, bf16[308,256]{1,0:T(8,128)(2,1)} %bitcast.7, ...), custom_call_target="tpu_custom_call" | custom-call | tf_op jit(solution)/shard_map/pallas_call | solution.py:526
  68.7 2.3 %shard_map.130 = (bf16[308,256]{1,0:T(8,128)(2,1)}, f32[64,512]{1,0:T(8,128)}, f32[4,308]{1,0:T(4,128)}, f32[1,1]{1,0:T(1,128)}) custom-call(bf16[308,256]{1,0:T(8,128)(2,1)} %get-tuple-element.12.refs_0_, f32[64,512]{1,0:T(8,128)} %get-tuple-element.13.refs_1_, f32[4,308]{1,0:T(4,128)} %get-tuple-element.14.refs_2_, f32[1,1]{1,0:T(1,128)} %get-tuple-element.15.refs_3_), custom_call_target="tpu_custom_call" | custom-call | tf_op jit(solution)/shard_map/pallas_call | solution.py:583

commit v4 on v3

--- a/solution.py
+++ b/solution.py
@@ -14,10 +14,11 @@
 M = 16
 TOP = 3
 MESH = pl.DeviceIdType.MESH
-ROWS = 320
-SPLIT = 256
-HALF = SPLIT // 2
+ROWS = 308
+SPLIT = 240
+CUTS = ((0, 128), (128, 112))
 REST = ROWS - SPLIT
+Q_CUTS = ((SPLIT, 32), (SPLIT + 32, REST - 32))
 F32 = jnp.float32
 BF16 = jnp.bfloat16
 
@@ -31,8 +32,10 @@
 
 
 def kernel(
-    x_hbm, w_ref, a_ref, up_ref, ups_ref, new_ref, old_ref, rew_ref, len_ref, asg_ref,
-    proj_ref, gdown_ref, gup_ref, loss_ref,
+    x_hbm, w_hbm, a_hbm, up_hbm, ups_hbm, new_hbm, old_hbm, rew_hbm, len_hbm, asg_hbm,
+    proj_hbm, gdown_hbm, gup_hbm, loss_hbm,
+    a_ref, up_ref, ups_ref, new_ref, old_ref, rew_ref, len_ref, asg_ref,
+    proj_ref, gdown_ref, gup_ref, loss_ref, in_sem, out_sem,
     xv, wg, acc, up_p, upt, og, row, tab, hs, hr, ag_a, red, rs, zx, ag, lows, gus, gur, gds, gdr, gda,
     x_sem, h_s, h_r, a_s, a_r, zs, xs, fs, w_r, qx_s, qx_r, qz_s, qz_r, r_s, r_r, z_s, z_r, g_s, g_r, u_s, u_r, d_s, d_r, e_s, e_r,
 ):
@@ -41,8 +44,7 @@
     z, x = lax.div(g, SIDE), lax.rem(g, SIDE)
     zh, i = lax.div(f, M), lax.rem(f, M)
     a, b = lax.div(i, SIDE), lax.rem(i, SIDE)
-    hidden = w_ref.shape[0]
-    cols = w_ref.shape[1]
+    hidden, cols = w_hbm.shape
 
     def copy(src, dst, ss, rr, tg, tf):
         return pltpu.make_async_remote_copy(
@@ -102,9 +104,6 @@
     def tx_in(d):
         j = top_from(d)
         return copy(zx.at[j], zx.at[j], z_s.at[d], z_r.at[d], g, j * M + i)
-
-    x_copy = pltpu.make_async_copy(x_hbm, xv, x_sem)
-    x_copy.start()
 
     barrier = pltpu.get_barrier_semaphore()
 
@@ -120,8 +119,34 @@
         TOP,
     )
 
-    wg[g, ROWS - 16 : ROWS, :] = jnp.zeros((16, cols), BF16)
-    wg[g, 0:hidden, :] = w_ref[...]
+    small = [
+        pltpu.make_async_copy(source, target, in_sem.at[at])
+        for at, (source, target) in enumerate(
+            (
+                (rew_hbm, rew_ref), (asg_hbm, asg_ref), (len_hbm, len_ref), (old_hbm, old_ref),
+                (new_hbm, new_ref), (up_hbm, up_ref), (a_hbm, a_ref), (ups_hbm, ups_ref),
+                (w_hbm, wg.at[g]),
+            )
+        )
+    ]
+    for c in small:
+        c.start()
+    x_copy = pltpu.make_async_copy(x_hbm, xv, x_sem)
+    x_copy.start()
+    outs = [
+        pltpu.make_async_copy(source, target, out_sem.at[at])
+        for at, (source, target) in enumerate(
+            (
+                (loss_ref, loss_hbm), (gup_ref, gup_hbm),
+                (gdown_ref, gdown_hbm), (proj_ref, proj_hbm),
+            )
+        )
+    ]
+    hs[...] = jnp.zeros(hs.shape, F32)
+    up_p[...] = jnp.zeros(up_p.shape, BF16)
+    og[...] = jnp.zeros(og.shape, BF16)
+    for c in small:
+        c.wait()
 
     rewards = rew_ref[...]
     mean = jnp.sum(rewards, axis=1, keepdims=True) / COMP
@@ -136,7 +161,6 @@
         sent_old = jnp.where(dest[:, k : k + 1], old[k : k + 1, :], sent_old)
     sent_adv = jnp.sum(jnp.where(dest, advantage, 0.0), axis=1, keepdims=True)
     sent_len = jnp.sum(jnp.where(dest, lengths, 0.0), axis=1, keepdims=True)
-    hs[...] = jnp.zeros(hs.shape, F32)
     for at, value in enumerate((sent_old, sent_adv, sent_len)):
         tab[...] = jnp.zeros(tab.shape, F32)
         tab[:, 0:N] = jnp.broadcast_to(value, (N, N))
@@ -147,10 +171,8 @@
     for j in range(N):
         row[0:1, j * N : (j + 1) * N] = new_ref[0, j : j + 1, :]
 
-    up_p[...] = jnp.zeros(up_p.shape, BF16)
     up_p[:, 0:hidden] = up_ref[...]
     upt[...] = up_p[...].astype(F32).T.astype(BF16)
-    og[...] = jnp.zeros(og.shape, BF16)
 
     pl.semaphore_wait(barrier, 2 * (N - 1) + TOP - 1)
 
@@ -176,7 +198,7 @@
     left = z * SIDE + lax.rem(x + SIDE - 1, SIDE)
 
     def part(s, h):
-        return wg.at[s, pl.ds(h * HALF, HALF), :]
+        return wg.at[s, pl.ds(*CUTS[h]), :]
 
     def wx(s, h, sem, tg):
         return copy(part(s, h), part(s, h), sem, w_r.at[s, h], tg, f)
@@ -240,7 +262,7 @@
         return wg.at[s, pl.ds(SPLIT, REST), :]
 
     def q_half(s, h):
-        return wg.at[s, pl.ds(SPLIT + h * (REST // 2), REST // 2), :]
+        return wg.at[s, pl.ds(*Q_CUTS[h]), :]
 
     def q_rows(zz):
         return wg.at[pl.ds(zz * SIDE, SIDE), pl.ds(SPLIT, REST), :]
@@ -317,6 +339,7 @@
     ratio = jnp.exp(row[0:1, :] - recv_old)
     coef = jnp.where(position < recv_len, -(recv_adv * ratio) / (recv_len * COMP), 0.0)
     loss_ref[...] = jnp.sum(coef, axis=1, keepdims=True)
+    outs[0].start()
     og[0:hidden, :] = (coef * ups_ref[...].astype(F32)).astype(BF16)
     back = dot_nn(up_p[...], og[...])
     for p in range(M):
@@ -461,6 +484,7 @@
     for j in range(1, N):
         total_up = total_up + gur[j]
     gup_ref[...] = total_up[:, 0:hidden]
+    outs[1].start()
 
     @pl.when(outer)
     def _():
@@ -470,8 +494,10 @@
     each(lambda d: sg_in(gda, e_s, e_r, d).wait_recv())
     for j in range(M):
         gdown_ref[j * 4 : (j + 1) * 4, :] = gda[j]
+    outs[2].start()
     finish(3)
-    proj_ref[...] = acc[0:hidden, :].astype(BF16)
+    proj_ref[...] = acc[...].astype(BF16)
+    outs[3].start()
 
     each(lambda d: gx(hs, hr, h_s, h_r, d).wait_send())
 
@@ -499,11 +525,21 @@
     each(lambda d: gx(gus, gur, u_s, u_r, d).wait_send())
     each(lambda d: gx(gds, gdr, d_s, d_r, d).wait_send())
     each(lambda d: sg(gda, e_s, e_r, d).wait_send())
+    for c in outs:
+        c.wait()
 
 
 def keep(*refs):
-    for taken, given in zip(refs[:4], refs[4:]):
-        given[...] = taken[...]
+    given, taken, held, come, go = refs[:4], refs[4:8], refs[8:12], refs[12], refs[13]
+    loads = [pltpu.make_async_copy(given[n], held[n], come.at[n]) for n in range(4)]
+    stores = [pltpu.make_async_copy(held[n], taken[n], go.at[n]) for n in range(4)]
+    for c in loads:
+        c.start()
+    for load, store in zip(loads, stores):
+        load.wait()
+        store.start()
+    for c in stores:
+        c.wait()
 
 
 def on_device(
@@ -521,7 +557,7 @@
     tokens, depth = hidden_input_slots.shape
     share, hidden = base_weight.shape
     rank = adapter_a.shape[1]
-    vmem = pl.BlockSpec(memory_space=pltpu.VMEM)
+    hbm = pl.BlockSpec(memory_space=pl.ANY)
     dma = pltpu.SemaphoreType.DMA
     projection, down, up, loss = pl.pallas_call(
         kernel,
@@ -531,9 +567,23 @@
             jax.ShapeDtypeStruct((rank // N, hidden), F32),
             jax.ShapeDtypeStruct((1, 1), F32),
         ),
-        in_specs=[pl.BlockSpec(memory_space=pl.ANY)] + [vmem] * 9,
-        out_specs=(vmem,) * 4,
+        in_specs=[hbm] * 10,
+        out_specs=(hbm,) * 4,
         scratch_shapes=[
+            pltpu.VMEM((rank, share), BF16),
+            pltpu.VMEM((rank, hidden), BF16),
+            pltpu.VMEM((hidden, tokens), BF16),
+            pltpu.VMEM(logp_new.shape, F32),
+            pltpu.VMEM(logp_old.shape, F32),
+            pltpu.VMEM(rewards.shape, F32),
+            pltpu.VMEM(comp_lengths.shape, jnp.int32),
+            pltpu.VMEM(assignment.shape, jnp.int32),
+            pltpu.VMEM((hidden, tokens), BF16),
+            pltpu.VMEM((rank, share), F32),
+            pltpu.VMEM((rank // N, hidden), F32),
+            pltpu.VMEM((1, 1), F32),
+            dma((9,)),
+            dma((4,)),
             pltpu.VMEM((tokens, depth), BF16),
             pltpu.VMEM((N, ROWS, share), BF16),
             pltpu.VMEM((ROWS, tokens), F32),
@@ -542,8 +592,8 @@
             pltpu.VMEM((384, tokens), BF16),
             pltpu.VMEM((8, tokens), F32),
             pltpu.VMEM((N, tokens), F32),
-            pltpu.VMEM((N, 8, tokens), F32),
-            pltpu.VMEM((N, 8, tokens), F32),
+            pltpu.VMEM((N, 4, tokens), F32),
+            pltpu.VMEM((N, 4, tokens), F32),
             pltpu.VMEM((SIDE, rank, 128), BF16),
             pltpu.VMEM((M, 8, tokens), F32),
             pltpu.VMEM((M, 8, tokens), F32),
@@ -580,14 +630,14 @@
         comp_lengths,
         assignment,
     )
+    made = (projection, down, up, loss)
     kept = pl.pallas_call(
         keep,
-        out_shape=tuple(
-            jax.ShapeDtypeStruct(v.shape, v.dtype) for v in (projection, down, up, loss)
-        ),
-        in_specs=[vmem] * 4,
-        out_specs=(vmem,) * 4,
-    )(projection, down, up, loss)
+        out_shape=tuple(jax.ShapeDtypeStruct(v.shape, v.dtype) for v in made),
+        in_specs=[hbm] * 4,
+        out_specs=(hbm,) * 4,
+        scratch_shapes=[pltpu.VMEM(v.shape, v.dtype) for v in made] + [dma((4,)), dma((4,))],
+    )(*made)
     projection, down, up, loss = kept
     return (projection.T, down.T, up, loss.reshape(1))
 

time: 71.1 us -> 71 us (level)
  no operation moved by 1% of the time
where the time goes in v4:
time: 71 us; the launch traced here: 70.9 us
  Pallas kernels  70.2 us (99%)
    pallas_call x1, Pallas kernels, on_device(): pl.pallas_call(kernel, out_shape=(jax.ShapeDtypeStruct((hidden, tokens),...  68 us
    pallas_call x1, Pallas kernels, on_device(): pl.pallas_call(keep, out_shape=tuple((jax.ShapeDtypeStruct(v.shape, v.dty...  2.27 us

profile of v4, /device:TPU:1, one launch (start us, length us, event | category | flops | bytes accessed | tf_op | source)
XLA Modules:
  0.0 70.9 jit_solution(12010566048189788351)
XLA Ops:
  0.6 68.0 %shard_map.129 = (bf16[308,256]{1,0:T(8,128)(2,1)}, f32[64,512]{1,0:T(8,128)}, f32[4,308]{1,0:T(4,128)}, f32[1,1]{1,0:T(1,128)}) custom-call(bf16[256,8192]{1,0:T(8,128)(2,1)} %x_hbm.1, bf16[308,512]{1,0:T(8,128)(2,1)} %bitcast.6, bf16[64,512]{1,0:T(8,128)(2,1)} %bitcast.8, bf16[64,308]{1,0:T(8,128)(2,1)} %up_hbm.1, bf16[308,256]{1,0:T(8,128)(2,1)} %bitcast.7, ...), custom_call_target="tpu_custom_call" | custom-call | tf_op jit(solution)/shard_map/pallas_call | solution.py:562
  68.6 2.3 %shard_map.130 = (bf16[308,256]{1,0:T(8,128)(2,1)}, f32[64,512]{1,0:T(8,128)}, f32[4,308]{1,0:T(4,128)}, f32[1,1]{1,0:T(1,128)}) custom-call(bf16[308,256]{1,0:T(8,128)(2,1)} %get-tuple-element.12.refs_0_, f32[64,512]{1,0:T(8,128)} %get-tuple-element.13.refs_1_, f32[4,308]{1,0:T(4,128)} %get-tuple-element.14.refs_2_, f32[1,1]{1,0:T(1,128)} %get-tuple-element.15.refs_3_), custom_call_target="tpu_custom_call" | custom-call | tf_op jit(solution)/shard_map/pallas_call | solution.py:634

commit v5 on v4

--- a/solution.py
+++ b/solution.py
@@ -15,8 +15,8 @@
 TOP = 3
 MESH = pl.DeviceIdType.MESH
 ROWS = 308
-SPLIT = 240
-CUTS = ((0, 128), (128, 112))
+SPLIT = 256
+CUTS = ((0, 128), (128, 128))
 REST = ROWS - SPLIT
 Q_CUTS = ((SPLIT, 32), (SPLIT + 32, REST - 32))
 F32 = jnp.float32
@@ -264,8 +264,8 @@
     def q_half(s, h):
         return wg.at[s, pl.ds(*Q_CUTS[h]), :]
 
-    def q_rows(zz):
-        return wg.at[pl.ds(zz * SIDE, SIDE), pl.ds(SPLIT, REST), :]
+    def q_rows(zz, e):
+        return wg.at[pl.ds(zz * SIDE + 2 * e, 2), pl.ds(SPLIT, REST), :]
 
     def q_send(go):
         go(q_copy(q_part(g), qx_s.at[0], qx_r.at[0], right))
@@ -276,25 +276,29 @@
         go(q_copy(q_half(shard(0, 1), 1), qx_s.at[3], qx_r.at[3], left))
 
     def q_first(go):
-        @pl.when(z < SIDE - 1)
-        def _():
-            go(q_copy(q_rows(z), qz_s.at[0], qz_r.at[z], g + SIDE))
-
-        @pl.when(z > 0)
-        def _():
-            go(q_copy(q_rows(z), qz_s.at[4], qz_r.at[z], g - SIDE))
-
-    def q_next(k, go):
-        go(q_copy(q_rows(near[k]), qz_s.at[k], qz_r.at[near[k]], beyond[k] * SIDE + x))
-
-    def q_land(k):
-        q_copy(q_rows(near[k]), qz_s.at[0], qz_r.at[near[k]], g).wait_recv()
+        for e in (0, 1):
+
+            @pl.when(z < SIDE - 1)
+            def _():
+                go(q_copy(q_rows(z, e), qz_s.at[0, e], qz_r.at[z, e], g + SIDE))
+
+            @pl.when(z > 0)
+            def _():
+                go(q_copy(q_rows(z, e), qz_s.at[4, e], qz_r.at[z, e], g - SIDE))
+
+    def q_next(k, e, go):
+        tg = beyond[k] * SIDE + x
+        go(q_copy(q_rows(near[k], e), qz_s.at[k, e], qz_r.at[near[k], e], tg))
+
+    def q_land(k, e):
+        q_copy(q_rows(near[k], e), qz_s.at[0, e], qz_r.at[near[k], e], g).wait_recv()
 
     def q_relay(k):
         @pl.when(inner)
         def _():
-            q_land(k)
-            q_next(k, start)
+            for e in (0, 1):
+                q_land(k, e)
+                q_next(k, e, start)
 
     def x_block(s):
         return xv[:, pl.ds(pl.multiple_of(s * cols, cols), cols)]
@@ -329,6 +333,24 @@
     q_send(start)
     z_first(start)
     x_send(0, start)
+
+    q_copy(q_part(shard(0, 3)), qx_s.at[0], qx_r.at[0], g).wait_recv()
+    q_copy(q_part(shard(0, 1)), qx_s.at[0], qx_r.at[1], g).wait_recv()
+    q_pass(start)
+    pass_on(0)
+    land(1)
+
+    @pl.when(inner)
+    def _():
+        z_next(1, start)
+
+    x_send(1, start)
+
+    @pl.when(inner)
+    def _():
+        land(2)
+        z_next(2, start)
+        x_send(2, start)
 
     each(lambda d: gx_in(hs, hr, h_s, h_r, d).wait_recv())
     got = hr[0]
@@ -345,9 +367,6 @@
     for p in range(M):
         red[p, 4:8, :] = back[p * 4 : (p + 1) * 4, :]
 
-    q_copy(q_part(shard(0, 3)), qx_s.at[0], qx_r.at[0], g).wait_recv()
-    q_copy(q_part(shard(0, 1)), qx_s.at[0], qx_r.at[1], g).wait_recv()
-    q_pass(start)
 
     def adapter(q, at_first):
         @pl.when((x != a) | (z != q))
@@ -376,22 +395,24 @@
     rs[i] = red[i]
     each(lambda d: sx(red, rs, r_s, r_r, d).start())
 
-    pass_on(0)
-    land(1)
+    q_copy(q_half(shard(0, 2), 0), qx_s.at[0], qx_r.at[2], g).wait_recv()
+    q_copy(q_half(shard(0, 2), 1), qx_s.at[0], qx_r.at[3], g).wait_recv()
+
+    @pl.when(outer)
+    def _():
+        q_first(start)
+
+    multiply(g, first=True)
 
     @pl.when(inner)
     def _():
-        z_next(1, start)
-
-    x_send(1, start)
-
-    @pl.when(inner)
+        land(3)
+        z_next(3, start)
+
+    @pl.when(outer)
     def _():
         land(2)
-        z_next(2, start)
         x_send(2, start)
-
-    multiply(g, first=True)
 
     each(lambda d: sx_in(red, rs, r_s, r_r, d).wait_recv())
     total = rs[0]
@@ -400,22 +421,12 @@
     zx[zh] = total
     each(lambda d: tx(d).start(), TOP)
 
-    q_copy(q_half(shard(0, 2), 0), qx_s.at[0], qx_r.at[2], g).wait_recv()
-    q_copy(q_half(shard(0, 2), 1), qx_s.at[0], qx_r.at[3], g).wait_recv()
-
     @pl.when(inner)
     def _():
-        land(3)
-        z_next(3, start)
-
-    q_first(start)
-
-    @pl.when(outer)
-    def _():
-        land(2)
-        x_send(2, start)
+        q_first(start)
 
     pass_on(1)
+    q_relay(1)
 
     each(lambda d: tx_in(d).wait_recv(), TOP)
     whole = zx[0] + zx[1] + zx[2]
@@ -440,7 +451,6 @@
         land(3)
 
     x_send(3, start)
-    q_relay(1)
     q_relay(2)
     finish(0)
     multiply(shard(1, 0))
@@ -456,6 +466,27 @@
     each(lambda d: gx(gus, gur, u_s, u_r, d).start())
 
     q_relay(3)
+
+    each(lambda d: gx(hs, hr, h_s, h_r, d).wait_send())
+
+    @pl.when(gives)
+    def _():
+        each(lambda d: ax(d).wait_send())
+
+    q_send(done)
+    q_pass(done)
+    z_first(done)
+
+    @pl.when(inner)
+    def _():
+        for k in range(1, SIDE):
+            z_next(k, done)
+
+    for k in (0, 1):
+        x_send(k, done)
+        x_pass(k, done)
+    each(lambda d: sx(red, rs, r_s, r_r, d).wait_send())
+    each(lambda d: tx(d).wait_send(), TOP)
     pass_on(3)
 
     each(lambda d: gx_in(gds, gdr, d_s, d_r, d).wait_recv())
@@ -475,7 +506,8 @@
 
         @pl.when(outer)
         def _():
-            q_land(k)
+            q_land(k, 0)
+            q_land(k, 1)
 
         q_multiply(k)
 
@@ -486,9 +518,23 @@
     gup_ref[...] = total_up[:, 0:hidden]
     outs[1].start()
 
+    q_first(done)
+
+    @pl.when(inner)
+    def _():
+        for e in (0, 1):
+            q_next(1, e, done)
+
+    x_send(2, done)
+    x_pass(2, done)
+    each(lambda d: sg(ag, g_s, g_r, d).wait_send())
+    each(lambda d: gx(gds, gdr, d_s, d_r, d).wait_send())
+    each(lambda d: gx(gus, gur, u_s, u_r, d).wait_send())
+
     @pl.when(outer)
     def _():
-        q_land(3)
+        q_land(3, 0)
+        q_land(3, 1)
 
     q_multiply(3)
     each(lambda d: sg_in(gda, e_s, e_r, d).wait_recv())
@@ -499,31 +545,14 @@
     proj_ref[...] = acc[...].astype(BF16)
     outs[3].start()
 
-    each(lambda d: gx(hs, hr, h_s, h_r, d).wait_send())
-
-    @pl.when(gives)
-    def _():
-        each(lambda d: ax(d).wait_send())
-
-    q_send(done)
-    q_pass(done)
-    q_first(done)
-    z_first(done)
-
     @pl.when(inner)
     def _():
-        for k in range(1, SIDE):
-            z_next(k, done)
-            q_next(k, done)
-
-    for k in range(SIDE):
-        x_send(k, done)
-        x_pass(k, done)
-    each(lambda d: sx(red, rs, r_s, r_r, d).wait_send())
-    each(lambda d: tx(d).wait_send(), TOP)
-    each(lambda d: sg(ag, g_s, g_r, d).wait_send())
-    each(lambda d: gx(gus, gur, u_s, u_r, d).wait_send())
-    each(lambda d: gx(gds, gdr, d_s, d_r, d).wait_send())
+        for k in (2, 3):
+            for e in (0, 1):
+                q_next(k, e, done)
+
+    x_send(3, done)
+    x_pass(3, done)
     each(lambda d: sg(gda, e_s, e_r, d).wait_send())
     for c in outs:
         c.wait()
@@ -609,7 +638,7 @@
             dma((N,)), dma((N,)),
             dma((N,)), dma((SIDE,)),
             dma((5, 2)), dma((SIDE, 2, 2)), dma((SIDE, 2)), dma((N, 2)),
-            dma((4,)), dma((4,)), dma((5,)), dma((SIDE,)),
+            dma((4,)), dma((4,)), dma((5, 2)), dma((SIDE, 2)),
             dma((M,)), dma((M,)),
             dma((TOP,)), dma((TOP,)),
             dma((M,)), dma((M,)),

time: 71 us -> 69 us (0.972)
  Pallas kernels: 70.2 us -> 68.2 us
    pallas_call x1, Pallas kernels: 68 us -> 65.9 us  [on_device(): pl.pallas_call(kernel, out_shape=(jax.ShapeDtypeStruct((hidden, tokens),...]
where the time goes in v5:
time: 69 us; the launch traced here: 68.8 us
  Pallas kernels  68.2 us (99%)
    pallas_call x1, Pallas kernels, on_device(): pl.pallas_call(kernel, out_shape=(jax.ShapeDtypeStruct((hidden, tokens),...  65.9 us
    pallas_call x1, Pallas kernels, on_device(): pl.pallas_call(keep, out_shape=tuple((jax.ShapeDtypeStruct(v.shape, v.dty...  2.27 us

profile of v5, /device:TPU:1, one launch (start us, length us, event | category | flops | bytes accessed | tf_op | source)
XLA Modules:
  0.0 68.8 jit_solution(14318013428592603482)
XLA Ops:
  0.6 65.9 %shard_map.129 = (bf16[308,256]{1,0:T(8,128)(2,1)}, f32[64,512]{1,0:T(8,128)}, f32[4,308]{1,0:T(4,128)}, f32[1,1]{1,0:T(1,128)}) custom-call(bf16[256,8192]{1,0:T(8,128)(2,1)} %x_hbm.1, bf16[308,512]{1,0:T(8,128)(2,1)} %bitcast.6, bf16[64,512]{1,0:T(8,128)(2,1)} %bitcast.8, bf16[64,308]{1,0:T(8,128)(2,1)} %up_hbm.1, bf16[308,256]{1,0:T(8,128)(2,1)} %bitcast.7, ...), custom_call_target="tpu_custom_call" | custom-call | tf_op jit(solution)/shard_map/pallas_call | solution.py:591
  66.5 2.3 %shard_map.130 = (bf16[308,256]{1,0:T(8,128)(2,1)}, f32[64,512]{1,0:T(8,128)}, f32[4,308]{1,0:T(4,128)}, f32[1,1]{1,0:T(1,128)}) custom-call(bf16[308,256]{1,0:T(8,128)(2,1)} %get-tuple-element.12.refs_0_, f32[64,512]{1,0:T(8,128)} %get-tuple-element.13.refs_1_, f32[4,308]{1,0:T(4,128)} %get-tuple-element.14.refs_2_, f32[1,1]{1,0:T(1,128)} %get-tuple-element.15.refs_3_), custom_call_target="tpu_custom_call" | custom-call | tf_op jit(solution)/shard_map/pallas_call | solution.py:663
